TPU v7x, 32 devices: a whole 2x2x4 slice. The times are simulated.
32 devices in a mesh: row: 4 (over z), col: 8 (over y, x, core).
Axes of the slice: x: 2, y: 2, z: 4, core: 2. Of those that a mesh axis runs over, the one named last changes fastest.
Arguments:
- dec_src: float32 [2304, 8192], P('col', 'row'), may hold values from -6 to 6
- enc_tgt: float32 [2304, 16384], P('row', 'col'), may hold values from -0.125 to 0.125
- src_coacts: float32 [512, 8192], P('col', 'row'), may hold values from -6 to 6
- tgt_coacts: float32 [512, 16384], P('row', 'col'), may hold values from -6 to 6
- eval_src: float32 [512, 8192], P('col', 'row'), may hold values from -6 to 6
- enc_bias: float32 [16384], P('col'), may hold values from -0.5 to 0.5
- dec_tgt: float32 [2304, 16384], P('row', 'col'), may hold values from -0.046875 to 0.046875
- tile_mask: int32 [128, 256], P('row', 'col'), may hold values from 0 to 1, as said below
Outputs:
- recon: float32 [512, 2304], P('col', 'row')
Inputs may be any that keep to these rules, and one draw needn't show every extreme that they name: `tile_mask`: 1 keeps a tile, 0 prunes it; the share of kept tiles differs between regions of the grid.
All inputs are finite; a program needn't handle non-finite values.
Results may differ from a plain program's by a relative error of at most 0.0003.
Values sent between devices are 32-bit elements; how exact they have to be, the bound alone decides.
A program may use at most 192 MiB of HBM per device.

v0:
```python
import jax
import jax.numpy as jnp
from jax import lax
from jax.sharding import PartitionSpec as P

S = 8192
TILE = 64
PRECISE = lax.Precision.HIGHEST


def contract_first(left, right):
    return lax.dot_general(
        left, right, (((0,), (0,)), ((), ())), precision=PRECISE, preferred_element_type=jnp.float32
    )


def local(dec_src, enc_tgt, src_coacts, tgt_coacts, eval_src, enc_bias, dec_tgt, tile_mask):
    src_count = dec_src.shape[1]
    tgt_count = enc_tgt.shape[1]
    enc_full = lax.all_gather(enc_tgt, "row", axis=0, tiled=True)
    src_full, eval_full = (
        lax.all_gather(src_coacts, "col", axis=0, tiled=True),
        lax.all_gather(eval_src, "col", axis=0, tiled=True),
    )
    virtual = contract_first(lax.all_gather(dec_src, "col", axis=0, tiled=True), enc_full)
    coact = contract_first(src_full, lax.all_gather(tgt_coacts, "row", axis=0, tiled=True))
    coact = coact * (1.0 / jnp.sqrt(jnp.float32(src_full.shape[0])))
    tile_rows, tile_cols = tile_mask.shape
    mask_float = tile_mask.astype(jnp.float32)
    weighted = (
        (virtual * coact).reshape(tile_rows, TILE, tile_cols, TILE) * mask_float[:, None, :, None]
    ).reshape(src_count, tgt_count)
    partial_pre = jnp.dot(
        eval_full, weighted, precision=PRECISE, preferred_element_type=jnp.float32
    )
    scale = 1.0 / jnp.sqrt(jnp.float32(S))
    pre_acts = lax.psum(partial_pre, "row")
    hidden = jnp.maximum(pre_acts * scale + enc_bias[None, :], 0.0)
    recon_part = lax.dot_general(
        hidden,
        dec_tgt,
        (((1,), (1,)), ((), ())),
        precision=PRECISE,
        preferred_element_type=jnp.float32,
    )
    return lax.psum_scatter(recon_part, "col", scatter_dimension=0, tiled=True)


def solution(mesh):
    return jax.shard_map(
        local,
        mesh=mesh,
        in_specs=(
            P("col", "row"),
            P("row", "col"),
            P("col", "row"),
            P("row", "col"),
            P("col", "row"),
            P("col"),
            P("row", "col"),
            P("row", "col"),
        ),
        out_specs=P("col", "row"),
        check_vma=False,
    )
```

profile of v0, /device:TPU:0, one launch (start us, length us, event | category | flops | bytes accessed | tf_op | source)
XLA Modules:
  0.0 963.4 jit_solution(13110801990855593298)
XLA Ops:
  6.5 0.0 copy-start
  6.5 0.0 all-gather.12.cloned.1.call-start
  6.5 0.7 all-gather.12.cloned.1.call-update
  7.3 0.0 all-gather.10.cloned.1.call-start
  7.3 0.7 all-gather.10.cloned.1.call-update
  8.0 0.0 all-gather.8.cloned.1.call-start
  8.1 0.7 all-gather.8.cloned.1.call-update
  8.7 0.0 all-gather.6.cloned.1.call-start
  8.8 0.5 all-gather.6.cloned.1.call-update
  9.3 0.0 all-gather.14.cloned.1.call-start
  9.4 0.5 all-gather.14.cloned.1.call-update
  9.9 0.0 all-reduce.2.cloned.1.call-start
  10.0 0.0 copy-done
  10.0 11.9 %mul.29 = f32[32,64,32,64]{3,2,1,0:T(8,128)} broadcast(f32[32,32]{1,0:T(8,128)S(1)} %convert_element_type.3), dimensions={0,2} | broadcast | bytes 16781312 | tf_op jit(solution)/shard_map/mul | solution.py:31
  21.9 29.0 %mul.30 = f32[2048,2048]{1,0:T(8,128)} reshape(f32[32,64,32,64]{3,2,1,0:T(8,128)} %mul.29) | data formatting | bytes 33554432 | tf_op jit(solution)/shard_map/mul | solution.py:31
  50.9 41.5 %all-gather.12.cloned.1.call-done = f32[512,2048]{1,0:T(8,128)} async-done(((f32[128,2048]{1,0:T(8,128)}), f32[512,2048]{1,0:T(8,128)}) %all-gather.12.cloned.1.call-update) | async-done | bytes 4194320 | tf_op jit(solution)/shard_map/all_gather | solution.py:26
  92.4 37.0 %all-gather.10.cloned.1.call-done = f32[512,2048]{1,0:T(8,128)} async-done(((f32[64,2048]{1,0:T(8,128)}), f32[512,2048]{1,0:T(8,128)}) %all-gather.10.cloned.1.call-update) | async-done | bytes 4194320 | tf_op jit(solution)/shard_map/all_gather | solution.py:22
  129.4 31.4 %fusion.19 = f32[2048,2048]{1,0:T(8,128)} fusion(f32[512,2048]{1,0:T(8,128)} %all-gather.10.cloned.1.call-done, f32[512,2048]{1,0:T(8,128)} %all-gather.12.cloned.1.call-done), kind=kOutput, calls=%fused_computation.17 | convolution fusion | flops 25769803776 | bytes 25165824 | tf_op jit(solution)/shard_map/dot_general | solution.py:12
  160.8 292.8 %all-gather.8.cloned.1.call-done = f32[2304,2048]{1,0:T(8,128)} async-done(((f32[576,2048]{1,0:T(8,128)}), f32[2304,2048]{1,0:T(8,128)}) %all-gather.8.cloned.1.call-update) | async-done | bytes 18874384 | tf_op jit(solution)/shard_map/all_gather | solution.py:20
  453.6 99.2 %all-gather.6.cloned.1.call-done = f32[2304,2048]{1,0:T(8,128)} async-done(((f32[288,2048]{1,0:T(8,128)}), f32[2304,2048]{1,0:T(8,128)}) %all-gather.6.cloned.1.call-update) | async-done | bytes 18874384 | tf_op jit(solution)/shard_map/all_gather | solution.py:25
  552.8 125.5 %fusion.18 = f32[2048,2048]{1,0:T(8,128)} fusion(f32[2304,2048]{1,0:T(8,128)} %all-gather.6.cloned.1.call-done, f32[2304,2048]{1,0:T(8,128)} %all-gather.8.cloned.1.call-done), kind=kOutput, calls=%fused_computation.16 | convolution fusion | flops 115964116992 | bytes 54525952 | tf_op jit(solution)/shard_map/dot_general | solution.py:12
  678.3 0.0 copy-start.1
  678.3 0.0 all-gather.14.cloned.1.call-done
  678.4 62.9 %fusion.9 = f32[512,2048]{0,1:T(8,128)} fusion(f32[512,2048]{1,0:T(8,128)} %all-gather.14.cloned.1.call-done, f32[2048,2048]{1,0:T(8,128)} %mul.30, f32[2048,2048]{1,0:T(8,128)} %fusion.18, f32[2048,2048]{1,0:T(8,128)} %fusion.19), kind=kOutput, calls=%fused_computation.9 | convolution fusion | flops 25782386688 | bytes 58720256 | tf_op jit(solution)/shard_map/dot_general | solution.py:33
  741.2 0.0 all-reduce.2.cloned.1.call-update
  741.3 0.0 reduce-scatter.2.cloned.1.call-start
  741.3 155.1 %all-reduce.2.cloned.1.call-done = f32[512,2048]{0,1:T(8,128)} async-done(((f32[512,2048]{0,1:T(8,128)}), f32[512,2048]{0,1:T(8,128)}) %all-reduce.2.cloned.1.call-update) | async-done | bytes 4194320 | tf_op jit(solution)/shard_map/psum | solution.py:37
  896.4 0.0 copy-done.1
  896.4 23.6 %fusion.5 = f32[512,576]{1,0:T(8,128)} fusion(f32[576,2048]{1,0:T(8,128)} %param.14, f32[512,2048]{0,1:T(8,128)} %all-reduce.2.cloned.1.call-done, f32[2048]{0:T(1024)S(1)} %copy-done.1), kind=kOutput, calls=%fused_computation.5 | convolution fusion | flops 7250903040 | bytes 10100736 | tf_op jit(solution)/shard_map/dot_general | solution.py:39
  920.1 0.0 reduce-scatter.2.cloned.1.call-update
  920.1 36.3 %reduce-scatter.2.cloned.1.call-done = f32[64,576]{1,0:T(8,128)} async-done(((f32[512,576]{1,0:T(8,128)}), f32[64,576]{1,0:T(8,128)}) %reduce-scatter.2.cloned.1.call-update) | async-done | bytes 147472 | tf_op jit(solution)/shard_map/reduce_scatter | solution.py:46
  (1 shorter events, 0.0 us)
Async XLA Ops:
  6.5 3.4 copy-start
  6.5 85.9 %all-gather.12.cloned.1.call-start = ((), (), s32[]{:S(2)}) async-start(), calls=%async_computation.4 | async-start | bytes 5242880 | tf_op jit(solution)/shard_map/all_gather | solution.py:26
  7.3 122.1 %all-gather.10.cloned.1.call-start = ((), (), s32[]{:S(2)}) async-start(), calls=%async_computation.3 | async-start | bytes 4718592 | tf_op jit(solution)/shard_map/all_gather | solution.py:22
  8.0 445.6 %all-gather.8.cloned.1.call-start = ((), (), s32[]{:S(2)}) async-start(), calls=%async_computation.2 | async-start | bytes 23592960 | tf_op jit(solution)/shard_map/all_gather | solution.py:20
  8.7 544.0 %all-gather.6.cloned.1.call-start = ((), (), s32[]{:S(2)}) async-start(), calls=%async_computation.1 | async-start | bytes 21233664 | tf_op jit(solution)/shard_map/all_gather | solution.py:25
  9.3 669.0 %all-gather.14.cloned.1.call-start = ((), (), s32[]{:S(2)}) async-start(), calls=%async_computation.5 | async-start | bytes 4718592 | tf_op jit(solution)/shard_map/all_gather | solution.py:23
  9.9 886.5 %all-reduce.2.cloned.1.call-start = ((), (), s32[]{:S(2)}) async-start(), calls=%async_computation.6 | async-start | bytes 8388608 | tf_op jit(solution)/shard_map/psum | solution.py:37
  678.3 218.1 %copy-start.1 = (f32[2048]{0:T(1024)S(1)}, f32[2048]{0:T(1024)}, u32[]{:S(2)}) copy-start(f32[2048]{0:T(1024)} %param.13) | copy-start | bytes 24580
  741.3 215.1 %reduce-scatter.2.cloned.1.call-start = ((), (), s32[]{:S(2)}) async-start(), calls=%async_computation.7 | async-start | bytes 1474560 | tf_op jit(solution)/shard_map/reduce_scatter | solution.py:46
Sparse Core Ops, SparseCore 0:
  8.9 83.4 all-gather.11
  94.3 35.0 all-gather.9
  131.0 322.5 all-gather.7
  455.3 97.4 all-gather.5
  554.5 36.5 all-gather.13
  741.4 154.9 all-reduce.1
  920.2 36.1 reduce-scatter.1
where the time goes:
time: 970 us; the launch traced here: 963 us
  waiting for transfers between devices  665 us (69%)
  matrix products  243 us (25%)
  local copies, waits for them, and re-layouts  40.9 us (4%)
  between operations  13.7 us (1%)
    all_gather x1, waiting for transfers between devices, local(): enc_full = lax.all_gather(enc_tgt, 'row', axis=0, tiled=True)  293 us
    dot_general x2, matrix products, contract_first(): lax.dot_general(left, right, (((0,), (0,)), ((), ())), precision=PRECISE,...  157 us
    psum x1, waiting for transfers between devices, local(): pre_acts = lax.psum(partial_pre, 'row')  155 us
    all_gather x1, waiting for transfers between devices, local(): lax.all_gather(dec_src, 'col', axis=0, tiled=True)  99.2 us
    dot_general x1, matrix products, local(): jnp.dot(eval_full, weighted, precision=PRECISE, preferred_element_type=jn...  62.9 us
    all_gather x1, waiting for transfers between devices, local(): lax.all_gather(tgt_coacts, 'row', axis=0, tiled=True)  41.5 us
    mul x2, local copies, waits for them, and re-layouts, local(): (virtual * coact).reshape(tile_rows, TILE, tile_cols, TILE)  40.9 us
    all_gather x1, waiting for transfers between devices, local(): lax.all_gather(src_coacts, 'col', axis=0, tiled=True)  37 us
  transfers between devices with their start and end apart: 7, of which 6 were waited for; matrix products, arithmetic and copies ran while one was open for 21% of the time, Pallas kernels for 0%

commit v1 on v0

--- a/solution.py
+++ b/solution.py
@@ -34,7 +34,7 @@
         eval_full, weighted, precision=PRECISE, preferred_element_type=jnp.float32
     )
     scale = 1.0 / jnp.sqrt(jnp.float32(S))
-    pre_acts = lax.psum(partial_pre, "row")
+    pre_acts = jnp.sum(lax.all_gather(partial_pre, "row"), axis=0)
     hidden = jnp.maximum(pre_acts * scale + enc_bias[None, :], 0.0)
     recon_part = lax.dot_general(
         hidden,

time: 970 us -> 1140 us (1.18)
  waiting for transfers between devices: 665 us -> 796 us
  local copies, waits for them, and re-layouts: 40.9 us -> 61.3 us
  other arithmetic: 0.01 us -> 16.1 us
    all_gather x0 -> x1, waiting for transfers between devices: none -> 287 us  [local(): pre_acts = jnp.sum(lax.all_gather(partial_pre, 'row'), axis=0)]
    psum x1 -> x0, waiting for transfers between devices: 155 us -> none  [local(): pre_acts = lax.psum(partial_pre, 'row')]
    all_gather x0 -> x1, local copies, waits for them, and re-layouts: none -> 20.4 us  [local(): pre_acts = jnp.sum(lax.all_gather(partial_pre, 'row'), axis=0)]
    reduce_sum x0 -> x1, other arithmetic: none -> 16.1 us  [local(): pre_acts = jnp.sum(lax.all_gather(partial_pre, 'row'), axis=0)]
  transfers between devices with their start and end apart: 7 -> 7, of which waited for: 6 -> 6; matrix products, arithmetic and copies ran while one was open for 21% -> 17% of each run, Pallas kernels for 0% -> 0%
where the time goes in v1:
time: 1140 us; the launch traced here: 1130 us
  waiting for transfers between devices  796 us (70%)
  matrix products  243 us (21%)
  local copies, waits for them, and re-layouts  61.3 us (5%)
  other arithmetic  16.1 us (1%)
  between operations  13.7 us (1%)
    all_gather x1, waiting for transfers between devices, local(): enc_full = lax.all_gather(enc_tgt, 'row', axis=0, tiled=True)  293 us
    all_gather x1, waiting for transfers between devices, local(): pre_acts = jnp.sum(lax.all_gather(partial_pre, 'row'), axis=0)  287 us
    dot_general x2, matrix products, contract_first(): lax.dot_general(left, right, (((0,), (0,)), ((), ())), precision=PRECISE,...  157 us
    all_gather x1, waiting for transfers between devices, local(): lax.all_gather(dec_src, 'col', axis=0, tiled=True)  99.2 us
    dot_general x1, matrix products, local(): jnp.dot(eval_full, weighted, precision=PRECISE, preferred_element_type=jn...  62.9 us
    all_gather x1, waiting for transfers between devices, local(): lax.all_gather(tgt_coacts, 'row', axis=0, tiled=True)  41.5 us
    mul x2, local copies, waits for them, and re-layouts, local(): (virtual * coact).reshape(tile_rows, TILE, tile_cols, TILE)  40.9 us
    all_gather x1, waiting for transfers between devices, local(): lax.all_gather(src_coacts, 'col', axis=0, tiled=True)  37 us
  transfers between devices with their start and end apart: 7, of which 6 were waited for; matrix products, arithmetic and copies ran while one was open for 17% of the time, Pallas kernels for 0%

profile of v1, /device:TPU:0, one launch (start us, length us, event | category | flops | bytes accessed | tf_op | source)
XLA Modules:
  0.0 1130.9 jit_solution(6221076987516872284)
XLA Ops:
  6.5 0.0 copy-start
  6.5 0.0 all-gather.14.cloned.1.call-start
  6.5 0.7 all-gather.14.cloned.1.call-update
  7.3 0.0 all-gather.12.cloned.1.call-start
  7.3 0.7 all-gather.12.cloned.1.call-update
  8.0 0.0 all-gather.10.cloned.1.call-start
  8.1 0.7 all-gather.10.cloned.1.call-update
  8.7 0.0 all-gather.8.cloned.1.call-start
  8.8 0.5 all-gather.8.cloned.1.call-update
  9.3 0.0 all-gather.16.cloned.1.call-start
  9.4 0.5 all-gather.16.cloned.1.call-update
  9.9 0.0 all-gather.18.cloned.1.call-start
  10.0 0.0 copy-done
  10.0 11.9 %mul.29 = f32[32,64,32,64]{3,2,1,0:T(8,128)} broadcast(f32[32,32]{1,0:T(8,128)S(1)} %convert_element_type.3), dimensions={0,2} | broadcast | bytes 16781312 | tf_op jit(solution)/shard_map/mul | solution.py:31
  21.9 29.0 %mul.30 = f32[2048,2048]{1,0:T(8,128)} reshape(f32[32,64,32,64]{3,2,1,0:T(8,128)} %mul.29) | data formatting | bytes 33554432 | tf_op jit(solution)/shard_map/mul | solution.py:31
  50.9 41.5 %all-gather.14.cloned.1.call-done = f32[512,2048]{1,0:T(8,128)} async-done(((f32[128,2048]{1,0:T(8,128)}), f32[512,2048]{1,0:T(8,128)}) %all-gather.14.cloned.1.call-update) | async-done | bytes 4194320 | tf_op jit(solution)/shard_map/all_gather | solution.py:26
  92.4 37.0 %all-gather.12.cloned.1.call-done = f32[512,2048]{1,0:T(8,128)} async-done(((f32[64,2048]{1,0:T(8,128)}), f32[512,2048]{1,0:T(8,128)}) %all-gather.12.cloned.1.call-update) | async-done | bytes 4194320 | tf_op jit(solution)/shard_map/all_gather | solution.py:22
  129.4 31.4 %fusion.19 = f32[2048,2048]{1,0:T(8,128)} fusion(f32[512,2048]{1,0:T(8,128)} %all-gather.12.cloned.1.call-done, f32[512,2048]{1,0:T(8,128)} %all-gather.14.cloned.1.call-done), kind=kOutput, calls=%fused_computation.17 | convolution fusion | flops 25769803776 | bytes 25165824 | tf_op jit(solution)/shard_map/dot_general | solution.py:12
  160.8 292.8 %all-gather.10.cloned.1.call-done = f32[2304,2048]{1,0:T(8,128)} async-done(((f32[576,2048]{1,0:T(8,128)}), f32[2304,2048]{1,0:T(8,128)}) %all-gather.10.cloned.1.call-update) | async-done | bytes 18874384 | tf_op jit(solution)/shard_map/all_gather | solution.py:20
  453.6 99.2 %all-gather.8.cloned.1.call-done = f32[2304,2048]{1,0:T(8,128)} async-done(((f32[288,2048]{1,0:T(8,128)}), f32[2304,2048]{1,0:T(8,128)}) %all-gather.8.cloned.1.call-update) | async-done | bytes 18874384 | tf_op jit(solution)/shard_map/all_gather | solution.py:25
  552.8 125.5 %fusion.18 = f32[2048,2048]{1,0:T(8,128)} fusion(f32[2304,2048]{1,0:T(8,128)} %all-gather.8.cloned.1.call-done, f32[2304,2048]{1,0:T(8,128)} %all-gather.10.cloned.1.call-done), kind=kOutput, calls=%fused_computation.16 | convolution fusion | flops 115964116992 | bytes 54525952 | tf_op jit(solution)/shard_map/dot_general | solution.py:12
  678.3 0.0 all-gather.16.cloned.1.call-done
  678.3 62.9 %fusion.9 = f32[512,2048]{0,1:T(8,128)} fusion(f32[512,2048]{1,0:T(8,128)} %all-gather.16.cloned.1.call-done, f32[2048,2048]{1,0:T(8,128)} %mul.30, f32[2048,2048]{1,0:T(8,128)} %fusion.18, f32[2048,2048]{1,0:T(8,128)} %fusion.19), kind=kOutput, calls=%fused_computation.9 | convolution fusion | flops 25782386688 | bytes 58720256 | tf_op jit(solution)/shard_map/dot_general | solution.py:33
  741.2 0.0 all-gather.18.cloned.1.call-update
  741.2 0.0 reduce-scatter.2.cloned.1.call-start
  741.3 286.9 %all-gather.18.cloned.1.call-done = f32[2048,2048]{0,1:T(8,128)} async-done(((f32[512,2048]{0,1:T(8,128)}), f32[2048,2048]{0,1:T(8,128)}) %all-gather.18.cloned.1.call-update) | async-done | bytes 16777232 | tf_op jit(solution)/shard_map/all_gather | solution.py:37
  1028.2 20.4 %reshape.5 = f32[4,512,2048]{1,0,2:T(4,128)} reshape(f32[2048,2048]{0,1:T(8,128)} %all-gather.18.cloned.1.call-done) | data formatting | bytes 33554432 | tf_op jit(solution)/shard_map/all_gather | solution.py:37
  1048.6 0.0 copy-start.1
  1048.6 16.1 %reduce_sum.9 = f32[512,2048]{0,1:T(8,128)} reduce(f32[4,512,2048]{1,0,2:T(4,128)} %reshape.5, f32[]{:T(128)} %constant.0.clone.1), dimensions={0}, to_apply=%region_0.0 | reduce | flops 3145728 | bytes 20971524 | tf_op jit(solution)/shard_map/reduce_sum | solution.py:37
  1064.7 0.0 copy-done.1
  1064.7 23.6 %fusion.5 = f32[512,576]{1,0:T(8,128)} fusion(f32[576,2048]{1,0:T(8,128)} %param.14, f32[512,2048]{0,1:T(8,128)} %reduce_sum.9, f32[2048]{0:T(1024)S(1)} %copy-done.1), kind=kOutput, calls=%fused_computation.5 | convolution fusion | flops 7250903040 | bytes 10100736 | tf_op jit(solution)/shard_map/dot_general | solution.py:39
  1088.3 0.0 reduce-scatter.2.cloned.1.call-update
  1088.3 35.5 %reduce-scatter.2.cloned.1.call-done = f32[64,576]{1,0:T(8,128)} async-done(((f32[512,576]{1,0:T(8,128)}), f32[64,576]{1,0:T(8,128)}) %reduce-scatter.2.cloned.1.call-update) | async-done | bytes 147472 | tf_op jit(solution)/shard_map/reduce_scatter | solution.py:46
  (1 shorter events, 0.0 us)
Async XLA Ops:
  6.5 3.4 copy-start
  6.5 85.9 %all-gather.14.cloned.1.call-start = ((), (), s32[]{:S(2)}) async-start(), calls=%async_computation.4 | async-start | bytes 5242880 | tf_op jit(solution)/shard_map/all_gather | solution.py:26
  7.3 122.1 %all-gather.12.cloned.1.call-start = ((), (), s32[]{:S(2)}) async-start(), calls=%async_computation.3 | async-start | bytes 4718592 | tf_op jit(solution)/shard_map/all_gather | solution.py:22
  8.0 445.6 %all-gather.10.cloned.1.call-start = ((), (), s32[]{:S(2)}) async-start(), calls=%async_computation.2 | async-start | bytes 23592960 | tf_op jit(solution)/shard_map/all_gather | solution.py:20
  8.7 544.1 %all-gather.8.cloned.1.call-start = ((), (), s32[]{:S(2)}) async-start(), calls=%async_computation.1 | async-start | bytes 21233664 | tf_op jit(solution)/shard_map/all_gather | solution.py:25
  9.3 669.0 %all-gather.16.cloned.1.call-start = ((), (), s32[]{:S(2)}) async-start(), calls=%async_computation.5 | async-start | bytes 4718592 | tf_op jit(solution)/shard_map/all_gather | solution.py:23
  9.9 1018.2 %all-gather.18.cloned.1.call-start = ((), (), s32[]{:S(2)}) async-start(), calls=%async_computation.7 | async-start | bytes 20971520 | tf_op jit(solution)/shard_map/all_gather | solution.py:37
  741.2 382.6 %reduce-scatter.2.cloned.1.call-start = ((), (), s32[]{:S(2)}) async-start(), calls=%async_computation.6 | async-start | bytes 1474560 | tf_op jit(solution)/shard_map/reduce_scatter | solution.py:46
  1048.6 16.1 %copy-start.1 = (f32[2048]{0:T(1024)S(1)}, f32[2048]{0:T(1024)}, u32[]{:S(2)}) copy-start(f32[2048]{0:T(1024)} %param.13) | copy-start | bytes 24580
Sparse Core Ops, SparseCore 0:
  8.9 83.4 all-gather.13
  94.3 35.0 all-gather.11
  131.0 322.5 all-gather.9
  455.3 97.4 all-gather.7
  554.5 36.5 all-gather.15
  741.4 286.7 all-gather.17
  1088.5 35.3 reduce-scatter.1
